TPU v7x, 256 devices: a whole 4x4x8 slice. The times are simulated.
256 devices in a mesh: gx: 16 (over z, core), gy: 16 (over x, y).
Axes of the slice: x: 4, y: 4, z: 8, core: 2. Of those that a mesh axis runs over, the one named last changes fastest.
Arguments:
- right_sides: float32 [16384, 8, 128], P(('gx', 'gy')), may hold values from -30 to 30
- diag_blocks: bfloat16 [16384, 128, 128], P(('gx', 'gy')), may hold values from -1 to 2
- face_blocks: bfloat16 [16384, 4, 128, 128], P(('gx', 'gy')), may hold values from -0.125 to 0.125
- neighbours: int32 [16384, 4], P(('gx', 'gy')), may hold values from -1 to 207, as said below
- send_slots: int32 [256, 9, 16], P(('gx', 'gy')), may hold values from -1 to 63, as said below
- counts: int32 [256], P(('gx', 'gy')), may hold values from 32 to 64, as said below
Outputs:
- solution: float32 [16384, 8, 128], P(('gx', 'gy'))
- residual: float32 [16384, 8, 128], P(('gx', 'gy'))
Inputs may be any that keep to these rules, and one draw needn't show every extreme that they name: The first counts[g] slots of group g hold its elements; some group has exactly 64. send_slots[g, d, k] is a live slot of group g whose vector group g sends, as its k-th ghost of direction d = 3 (dx + 1) + (dy + 1), to the group at grid offset (dx, dy); -1 marks no block. A list's live entries come first and are distinct; direction 4 and directions leaving the grid hold only -1; some list holds 16 live entries. neighbours[e, f] is -1 (no coupling), a live slot of the same group, or 64 + d * 16 + k naming a live entry k of direction d of the sending group at offset -(dx, dy); slots at or beyond counts hold only -1.
All inputs are finite; a program needn't handle non-finite values.
Results may differ from a plain program's by a relative error of at most 0.0075.
The roundings to bfloat16 on the way count: a program that leaves them out, or rounds other values in their place, can miss the bound.
Values may be sent and summed in bfloat16 or wider, within the bound.
No kernel may reach another device: no remote copies, remote signals or barrier semaphores. Data moves between devices by JAX's collectives and lax.ppermute only.
A program may use at most 64 MiB of HBM per device.

v0:
```python
import jax
import jax.numpy as jnp
from jax import lax
from jax.sharding import PartitionSpec as P

POWERS = 4
HIGH = lax.Precision.HIGHEST


def passed_along(block, axis, distance):
    devices = range(lax.axis_size(axis))
    route = [(i - distance, i) for i in devices if i - distance in devices]
    return lax.ppermute(block, axis, route)


def forward_solve(factor, values):
    extent = factor.shape[-1]
    result = []
    for row_at in range(extent):
        running = values[:, row_at]
        for col_at in range(row_at):
            running = running - factor[:, row_at, col_at] * result[col_at]
        result.append(running / factor[:, row_at, row_at])
    return jnp.stack(result, axis=1)


def backward_solve(factor, values):
    extent = factor.shape[-1]
    result = [None] * extent
    for row_at in reversed(range(extent)):
        running = values[:, row_at]
        for col_at in range(row_at + 1, extent):
            running = running - factor[:, col_at, row_at] * result[col_at]
        result[row_at] = running / factor[:, row_at, row_at]
    return jnp.stack(result, axis=1)


def coefficients(gram):
    factor = jnp.linalg.cholesky(gram[:, 1:, 1:])
    return backward_solve(factor, forward_solve(factor, gram[:, 1:, 0]))


def fetch_ghosts(packets):
    empty = jnp.zeros_like(packets[4])
    columns = lax.axis_size("gy")
    column = lax.axis_index("gy")
    arrived = []
    for target in range(9):
        if target == 4:
            arrived.append(empty)
        else:
            step_row = target // 3 - 1
            step_col = target % 3 - 1
            shifted = passed_along(packets[target], ("gx", "gy"), step_row * columns + step_col)
            inside = (column - step_col >= 0) & (column - step_col < columns)
            arrived.append(jnp.where(inside, shifted, jnp.zeros((), jnp.bfloat16)))
    return jnp.stack(arrived)


def per_device(right_sides, diag_blocks, face_blocks, neighbours, send_slots, counts):
    capacity = right_sides.shape[0]
    slot_ids = lax.iota(jnp.int32, capacity)
    live_mask = (slot_ids < counts[0]).astype(jnp.float32)[:, None, None]
    outgoing = send_slots[0]
    sending = outgoing >= 0
    out_index = jnp.where(sending, outgoing, 0)
    present = neighbours >= 0
    source = jnp.where(present, neighbours, 0)
    zero_half = jnp.zeros((), jnp.bfloat16)
    vectors = [right_sides * live_mask]
    for step_index in range(POWERS):
        rounded = vectors[-1].astype(jnp.bfloat16)
        packets = jnp.where(sending[:, :, None, None], rounded[out_index], zero_half)
        ghosts = fetch_ghosts(packets)
        lookup = jnp.concatenate([rounded, ghosts.reshape((-1,) + rounded.shape[1:])], axis=0)
        gathered = jnp.where(present[:, :, None, None], lookup[source], zero_half)
        own_part = jnp.einsum(
            "eij,erj->eri", diag_blocks, rounded, preferred_element_type=jnp.float32
        )
        face_part = jnp.einsum(
            "efij,efrj->eri", face_blocks, gathered, preferred_element_type=jnp.float32
        )
        vectors.append((own_part + face_part) * live_mask)
    basis = jnp.stack(vectors)
    local_gram = jnp.einsum("icrn,jcrn->rij", basis, basis, precision=HIGH)
    gram = lax.psum(local_gram, ("gx", "gy"))
    weights = coefficients(gram)
    solution = jnp.einsum("rk,kcrn->crn", weights, basis[:POWERS], precision=HIGH)
    residual = basis[0] - jnp.einsum("rk,kcrn->crn", weights, basis[1:], precision=HIGH)
    return (solution, residual)


def solution(mesh):
    in_specs = (
        P(("gx", "gy"), None, None),
        P(("gx", "gy"), None, None),
        P(("gx", "gy"), None, None, None),
        P(("gx", "gy"), None),
        P(("gx", "gy"), None, None),
        P(("gx", "gy")),
    )
    out_specs = (P(("gx", "gy"), None, None), P(("gx", "gy"), None, None))
    return jax.shard_map(
        per_device, mesh=mesh, in_specs=in_specs, out_specs=out_specs, check_vma=False
    )
```

profile of v0, /device:TPU:1, one launch (start us, length us, event | category | flops | bytes accessed | tf_op | source)
XLA Modules:
  0.0 309.1 jit_solution(4113129172325548190)
XLA Ops:
  7.9 5.1 %collective-permute-start.1 = (bf16[16,8,128]{2,1,0:T(8,128)(2,1)}, bf16[16,8,128]{2,1,0:T(8,128)(2,1)}, u32[]{:S(2)}, u32[]{:S(2)}) collective-permute-start(bf16[16,8,128]{2,1,0:T(8,128)(2,1)} %get-tuple-element.53), channel_id=1, source_target_pairs={{16,0},{17,1},{18,2},{19,3},{20,4},{21,5},{22,6},{23,7},{24,8},{25... | collective-permute-start | bytes 98312 | tf_op jit(solution)/shard_map/ppermute | solution.py:13
  13.1 1.9 collective-permute-start.2
  15.0 6.2 %collective-permute-start.3 = (bf16[16,8,128]{2,1,0:T(8,128)(2,1)}, bf16[16,8,128]{2,1,0:T(8,128)(2,1)}, u32[]{:S(2)}, u32[]{:S(2)}) collective-permute-start(bf16[16,8,128]{2,1,0:T(8,128)(2,1)} %get-tuple-element.51), channel_id=1, source_target_pairs={{1,0},{2,1},{3,2},{4,3},{5,4},{6,5},{7,6},{8,7},{9,8},{10,9},{11,1... | collective-permute-start | bytes 98312 | tf_op jit(solution)/shard_map/ppermute | solution.py:13
  21.2 1.9 collective-permute-start.4
  23.2 1.8 constant_dynamic-update-slice_fusion.40
  26.2 8.3 %collective-permute-start.5 = (bf16[16,8,128]{2,1,0:T(8,128)(2,1)}, bf16[16,8,128]{2,1,0:T(8,128)(2,1)S(1)}, u32[]{:S(2)}, u32[]{:S(2)}) collective-permute-start(bf16[16,8,128]{2,1,0:T(8,128)(2,1)} %get-tuple-element.49), channel_id=1, source_target_pairs={{0,15},{1,16},{2,17},{3,18},{4,19},{5,20},{6,21},{7,22},{8,23},{9,... | collective-permute-start | bytes 98312 | tf_op jit(solution)/shard_map/ppermute | solution.py:13
  35.3 6.7 %collective-permute-start.6 = (bf16[16,8,128]{2,1,0:T(8,128)(2,1)}, bf16[16,8,128]{2,1,0:T(8,128)(2,1)S(1)}, u32[]{:S(2)}, u32[]{:S(2)}) collective-permute-start(bf16[16,8,128]{2,1,0:T(8,128)(2,1)} %get-tuple-element.48), channel_id=1, source_target_pairs={{0,16},{1,17},{2,18},{3,19},{4,20},{5,21},{6,22},{7,23},{8,24},{9,... | collective-permute-start | bytes 98312 | tf_op jit(solution)/shard_map/ppermute | solution.py:13
  46.3 2.6 gather_fusion.1
  48.9 5.9 %convolution_bitcast_fusion.3 = f32[64,8,128]{2,1,0:T(8,128)S(1)} fusion(bf16[64,4,128,128]{3,2,1,0:T(8,128)(2,1)} %param.8, bf16[64,4,8,128]{3,2,1,0:T(8,128)(2,1)} %bitcast.295, pred[64,4]{1,0:T(8,128)(4,1)S(1)} %copy.36), kind=kOutput, calls=%fused_computation.20 | convolution fusion | flops 67371008 | bytes 9175296 | tf_op jit(solution)/shard_map/efij,efrj->eri/dot_general | solution.py:80
  56.7 1.4 gather_fusion.2
  59.4 1.3 collective-permute-start.8
  60.7 1.9 collective-permute-start.9
  62.6 1.9 collective-permute-start.10
  64.5 8.1 %collective-permute-start.11 = (bf16[16,8,128]{2,1,0:T(8,128)(2,1)S(1)}, bf16[16,8,128]{2,1,0:T(8,128)(2,1)S(1)}, u32[]{:S(2)}, u32[]{:S(2)}) collective-permute-start(bf16[16,8,128]{2,1,0:T(8,128)(2,1)S(1)} %get-tuple-element.43), channel_id=1, source_target_pairs={{1,0},{2,1},{3,2},{4,3},{5,4},{6,5},{7,6},{8,7},{9,8},{10,9},{11,1... | collective-permute-start | bytes 98312 | tf_op jit(solution)/shard_map/ppermute | solution.py:13
  72.6 1.9 collective-permute-start.12
  74.5 9.5 %collective-permute-start.13 = (bf16[16,8,128]{2,1,0:T(8,128)(2,1)S(1)}, bf16[16,8,128]{2,1,0:T(8,128)(2,1)S(1)}, u32[]{:S(2)}, u32[]{:S(2)}) collective-permute-start(bf16[16,8,128]{2,1,0:T(8,128)(2,1)S(1)} %get-tuple-element.41), channel_id=1, source_target_pairs={{0,15},{1,16},{2,17},{3,18},{4,19},{5,20},{6,21},{7,22},{8,23},{9,... | collective-permute-start | bytes 98312 | tf_op jit(solution)/shard_map/ppermute | solution.py:13
  84.1 7.8 %collective-permute-start.14 = (bf16[16,8,128]{2,1,0:T(8,128)(2,1)S(1)}, bf16[16,8,128]{2,1,0:T(8,128)(2,1)S(1)}, u32[]{:S(2)}, u32[]{:S(2)}) collective-permute-start(bf16[16,8,128]{2,1,0:T(8,128)(2,1)S(1)} %get-tuple-element.40), channel_id=1, source_target_pairs={{0,16},{1,17},{2,18},{3,19},{4,20},{5,21},{6,22},{7,23},{8,24},{9,... | collective-permute-start | bytes 98312 | tf_op jit(solution)/shard_map/ppermute | solution.py:13
  91.9 1.3 collective-permute-start.15
  95.0 2.6 gather_fusion.3
  97.6 5.9 %convolution_bitcast_fusion.2 = f32[64,8,128]{2,1,0:T(8,128)S(1)} fusion(bf16[64,4,128,128]{3,2,1,0:T(8,128)(2,1)} %param.8, bf16[64,4,8,128]{3,2,1,0:T(8,128)(2,1)} %bitcast.296, pred[64,4]{1,0:T(8,128)(4,1)S(1)} %copy.36), kind=kOutput, calls=%fused_computation.17 | convolution fusion | flops 67371008 | bytes 9175296 | tf_op jit(solution)/shard_map/efij,efrj->eri/dot_general | solution.py:80
  105.4 1.4 gather_fusion.4
  108.0 1.3 collective-permute-start.16
  109.8 1.9 collective-permute-start.17
  111.8 1.9 collective-permute-start.18
  113.7 8.1 %collective-permute-start.19 = (bf16[16,8,128]{2,1,0:T(8,128)(2,1)S(1)}, bf16[16,8,128]{2,1,0:T(8,128)(2,1)S(1)}, u32[]{:S(2)}, u32[]{:S(2)}) collective-permute-start(bf16[16,8,128]{2,1,0:T(8,128)(2,1)S(1)} %get-tuple-element.35), channel_id=1, source_target_pairs={{1,0},{2,1},{3,2},{4,3},{5,4},{6,5},{7,6},{8,7},{9,8},{10,9},{11,1... | collective-permute-start | bytes 98312 | tf_op jit(solution)/shard_map/ppermute | solution.py:13
  121.8 1.9 collective-permute-start.20
  123.7 9.5 %collective-permute-start.21 = (bf16[16,8,128]{2,1,0:T(8,128)(2,1)S(1)}, bf16[16,8,128]{2,1,0:T(8,128)(2,1)S(1)}, u32[]{:S(2)}, u32[]{:S(2)}) collective-permute-start(bf16[16,8,128]{2,1,0:T(8,128)(2,1)S(1)} %get-tuple-element.33), channel_id=1, source_target_pairs={{0,15},{1,16},{2,17},{3,18},{4,19},{5,20},{6,21},{7,22},{8,23},{9,... | collective-permute-start | bytes 98312 | tf_op jit(solution)/shard_map/ppermute | solution.py:13
  133.3 7.8 %collective-permute-start.22 = (bf16[16,8,128]{2,1,0:T(8,128)(2,1)S(1)}, bf16[16,8,128]{2,1,0:T(8,128)(2,1)S(1)}, u32[]{:S(2)}, u32[]{:S(2)}) collective-permute-start(bf16[16,8,128]{2,1,0:T(8,128)(2,1)S(1)} %get-tuple-element.32), channel_id=1, source_target_pairs={{0,16},{1,17},{2,18},{3,19},{4,20},{5,21},{6,22},{7,23},{8,24},{9,... | collective-permute-start | bytes 98312 | tf_op jit(solution)/shard_map/ppermute | solution.py:13
  144.3 2.6 gather_fusion.5
  146.9 5.9 %convolution_bitcast_fusion.1 = f32[64,8,128]{2,1,0:T(8,128)S(1)} fusion(bf16[64,4,128,128]{3,2,1,0:T(8,128)(2,1)} %param.8, bf16[64,4,8,128]{3,2,1,0:T(8,128)(2,1)} %bitcast.297, pred[64,4]{1,0:T(8,128)(4,1)S(1)} %copy.36), kind=kOutput, calls=%fused_computation.14 | convolution fusion | flops 67371008 | bytes 9175296 | tf_op jit(solution)/shard_map/efij,efrj->eri/dot_general | solution.py:80
  154.7 1.4 gather_fusion.6
  157.3 1.3 collective-permute-start.24
  159.1 1.9 collective-permute-start.25
  161.0 1.9 collective-permute-start.26
  162.9 8.2 %collective-permute-start.27 = (bf16[16,8,128]{2,1,0:T(8,128)(2,1)S(1)}, bf16[16,8,128]{2,1,0:T(8,128)(2,1)S(1)}, u32[]{:S(2)}, u32[]{:S(2)}) collective-permute-start(bf16[16,8,128]{2,1,0:T(8,128)(2,1)S(1)} %get-tuple-element.27), channel_id=1, source_target_pairs={{1,0},{2,1},{3,2},{4,3},{5,4},{6,5},{7,6},{8,7},{9,8},{10,9},{11,1... | collective-permute-start | bytes 98312 | tf_op jit(solution)/shard_map/ppermute | solution.py:13
  171.1 1.9 collective-permute-start.28
  173.0 9.6 %collective-permute-start.29 = (bf16[16,8,128]{2,1,0:T(8,128)(2,1)S(1)}, bf16[16,8,128]{2,1,0:T(8,128)(2,1)S(1)}, u32[]{:S(2)}, u32[]{:S(2)}) collective-permute-start(bf16[16,8,128]{2,1,0:T(8,128)(2,1)S(1)} %get-tuple-element.25), channel_id=1, source_target_pairs={{0,15},{1,16},{2,17},{3,18},{4,19},{5,20},{6,21},{7,22},{8,23},{9,... | collective-permute-start | bytes 98312 | tf_op jit(solution)/shard_map/ppermute | solution.py:13
  182.7 7.8 %collective-permute-start.30 = (bf16[16,8,128]{2,1,0:T(8,128)(2,1)S(1)}, bf16[16,8,128]{2,1,0:T(8,128)(2,1)S(1)}, u32[]{:S(2)}, u32[]{:S(2)}) collective-permute-start(bf16[16,8,128]{2,1,0:T(8,128)(2,1)S(1)} %get-tuple-element.24), channel_id=1, source_target_pairs={{0,16},{1,17},{2,18},{3,19},{4,20},{5,21},{6,22},{7,23},{8,24},{9,... | collective-permute-start | bytes 98312 | tf_op jit(solution)/shard_map/ppermute | solution.py:13
  190.5 1.5 collective-permute-start.31
  193.6 2.6 gather_fusion.7
  196.2 5.9 %convolution_bitcast_fusion = f32[64,8,128]{2,1,0:T(8,128)S(1)} fusion(bf16[64,4,128,128]{3,2,1,0:T(8,128)(2,1)} %param.8, bf16[64,4,8,128]{3,2,1,0:T(8,128)(2,1)} %bitcast.294, pred[64,4]{1,0:T(8,128)(4,1)S(1)} %copy.36), kind=kOutput, calls=%fused_computation.10 | convolution fusion | flops 67371008 | bytes 9175296 | tf_op jit(solution)/shard_map/efij,efrj->eri/dot_general | solution.py:80
  202.1 1.9 constant_dynamic-update-slice_fusion.36
  204.0 4.9 %fusion.7 = f32[8,5,5]{1,2,0:T(8,128)S(1)} fusion(f32[5,64,8,128]{3,2,1,0:T(8,128)S(1)} %get-tuple-element.61), kind=kOutput, calls=%fused_computation.23 | convolution fusion | flops 19660800 | bytes 1311520 | tf_op jit(solution)/shard_map/icrn,jcrn->rij/dot_general | solution.py:85
  209.0 87.5 %psum.7 = f32[8,5,5]{1,2,0:T(8,128)S(1)} all-reduce(f32[8,5,5]{1,2,0:T(8,128)S(1)} %fusion.7), channel_id=1, replica_groups=mesh['gx'=16,'gy'=16] {'gx','gy'}, use_global_device_ids=true, to_apply=%region_0.1 | all-reduce | flops 200 | bytes 1600 | tf_op jit(solution)/shard_map/psum | solution.py:86
  296.9 3.0 custom-call.4
  300.6 1.7 pad_maximum_fusion.1
  302.3 2.5 fusion.12
  305.7 2.5 fusion.10
  (148 shorter events, 32.5 us)
Async XLA Ops:
  0.6 54.1 %copy-start = (bf16[64,128,128]{2,1,0:T(8,128)(2,1)S(1)}, bf16[64,128,128]{2,1,0:T(8,128)(2,1)}, u32[]{:S(2)}) copy-start(bf16[64,128,128]{2,1,0:T(8,128)(2,1)} %param.7) | copy-start | bytes 6291460
  0.6 24.3 %copy-start.11 = (s32[64,4]{0,1:T(4,128)S(1)}, s32[64,4]{0,1:T(4,128)}, u32[]{:S(2)}) copy-start(s32[64,4]{0,1:T(4,128)} %param.9) | copy-start | bytes 3076
  2.9 22.6 %copy-start.6 = (f32[64]{0:T(128)}, f32[64]{0:T(128)S(1)}, u32[]{:S(2)}) copy-start(f32[64]{0:T(128)S(1)} %compare_convert_fusion) | copy-start | bytes 772
  3.9 17.3 %copy-start.5 = (pred[1,9,16]{2,1,0:T(8,128)(4,1)}, pred[1,9,16]{2,1,0:T(8,128)(4,1)S(1)}, u32[]{:S(2)}) copy-start(pred[1,9,16]{2,1,0:T(8,128)(4,1)S(1)} %copy.69) | copy-start | bytes 436
  6.6 19.6 %collective-permute-start = (bf16[16,8,128]{2,1,0:T(8,128)(2,1)}, bf16[16,8,128]{2,1,0:T(8,128)(2,1)}, u32[]{:S(2)}, u32[]{:S(2)}) collective-permute-start(bf16[16,8,128]{2,1,0:T(8,128)(2,1)} %get-tuple-element.54), channel_id=1, source_target_pairs={{17,0},{18,1},{19,2},{20,3},{21,4},{22,5},{23,6},{24,7},{25,8},{26... | collective-permute-start | bytes 98312 | tf_op jit(solution)/shard_map/ppermute | solution.py:13
  7.9 27.4 %collective-permute-start.1 = (bf16[16,8,128]{2,1,0:T(8,128)(2,1)}, bf16[16,8,128]{2,1,0:T(8,128)(2,1)}, u32[]{:S(2)}, u32[]{:S(2)}) collective-permute-start(bf16[16,8,128]{2,1,0:T(8,128)(2,1)} %get-tuple-element.53), channel_id=1, source_target_pairs={{16,0},{17,1},{18,2},{19,3},{20,4},{21,5},{22,6},{23,7},{24,8},{25... | collective-permute-start | bytes 98312 | tf_op jit(solution)/shard_map/ppermute | solution.py:13
  13.1 29.8 %collective-permute-start.2 = (bf16[16,8,128]{2,1,0:T(8,128)(2,1)}, bf16[16,8,128]{2,1,0:T(8,128)(2,1)}, u32[]{:S(2)}, u32[]{:S(2)}) collective-permute-start(bf16[16,8,128]{2,1,0:T(8,128)(2,1)} %get-tuple-element.52), channel_id=1, source_target_pairs={{15,0},{16,1},{17,2},{18,3},{19,4},{20,5},{21,6},{22,7},{23,8},{24... | collective-permute-start | bytes 98312 | tf_op jit(solution)/shard_map/ppermute | solution.py:13
  15.0 29.2 %collective-permute-start.3 = (bf16[16,8,128]{2,1,0:T(8,128)(2,1)}, bf16[16,8,128]{2,1,0:T(8,128)(2,1)}, u32[]{:S(2)}, u32[]{:S(2)}) collective-permute-start(bf16[16,8,128]{2,1,0:T(8,128)(2,1)} %get-tuple-element.51), channel_id=1, source_target_pairs={{1,0},{2,1},{3,2},{4,3},{5,4},{6,5},{7,6},{8,7},{9,8},{10,9},{11,1... | collective-permute-start | bytes 98312 | tf_op jit(solution)/shard_map/ppermute | solution.py:13
  21.2 23.8 %collective-permute-start.4 = (bf16[16,8,128]{2,1,0:T(8,128)(2,1)}, bf16[16,8,128]{2,1,0:T(8,128)(2,1)}, u32[]{:S(2)}, u32[]{:S(2)}) collective-permute-start(bf16[16,8,128]{2,1,0:T(8,128)(2,1)} %get-tuple-element.50), channel_id=1, source_target_pairs={{0,1},{1,2},{2,3},{3,4},{4,5},{5,6},{6,7},{7,8},{8,9},{9,10},{10,1... | collective-permute-start | bytes 98312 | tf_op jit(solution)/shard_map/ppermute | solution.py:13
  26.2 18.8 %collective-permute-start.5 = (bf16[16,8,128]{2,1,0:T(8,128)(2,1)}, bf16[16,8,128]{2,1,0:T(8,128)(2,1)S(1)}, u32[]{:S(2)}, u32[]{:S(2)}) collective-permute-start(bf16[16,8,128]{2,1,0:T(8,128)(2,1)} %get-tuple-element.49), channel_id=1, source_target_pairs={{0,15},{1,16},{2,17},{3,18},{4,19},{5,20},{6,21},{7,22},{8,23},{9,... | collective-permute-start | bytes 98312 | tf_op jit(solution)/shard_map/ppermute | solution.py:13
  35.3 9.8 %collective-permute-start.6 = (bf16[16,8,128]{2,1,0:T(8,128)(2,1)}, bf16[16,8,128]{2,1,0:T(8,128)(2,1)S(1)}, u32[]{:S(2)}, u32[]{:S(2)}) collective-permute-start(bf16[16,8,128]{2,1,0:T(8,128)(2,1)} %get-tuple-element.48), channel_id=1, source_target_pairs={{0,16},{1,17},{2,18},{3,19},{4,20},{5,21},{6,22},{7,23},{8,24},{9,... | collective-permute-start | bytes 98312 | tf_op jit(solution)/shard_map/ppermute | solution.py:13
  42.9 2.6 collective-permute-start.7
  48.9 5.9 %copy-start.7 = (f32[64]{0:T(128)S(1)}, f32[64]{0:T(128)}, u32[]{:S(2)}) copy-start(f32[64]{0:T(128)} %copy-done.6) | copy-start | bytes 772
  56.0 0.7 copy-start.2
  59.4 15.2 %collective-permute-start.8 = (bf16[16,8,128]{2,1,0:T(8,128)(2,1)S(1)}, bf16[16,8,128]{2,1,0:T(8,128)(2,1)S(1)}, u32[]{:S(2)}, u32[]{:S(2)}) collective-permute-start(bf16[16,8,128]{2,1,0:T(8,128)(2,1)S(1)} %get-tuple-element.46), channel_id=1, source_target_pairs={{17,0},{18,1},{19,2},{20,3},{21,4},{22,5},{23,6},{24,7},{25,8},{26... | collective-permute-start | bytes 98312 | tf_op jit(solution)/shard_map/ppermute | solution.py:13
  60.7 23.4 %collective-permute-start.9 = (bf16[16,8,128]{2,1,0:T(8,128)(2,1)S(1)}, bf16[16,8,128]{2,1,0:T(8,128)(2,1)S(1)}, u32[]{:S(2)}, u32[]{:S(2)}) collective-permute-start(bf16[16,8,128]{2,1,0:T(8,128)(2,1)S(1)} %get-tuple-element.45), channel_id=1, source_target_pairs={{16,0},{17,1},{18,2},{19,3},{20,4},{21,5},{22,6},{23,7},{24,8},{25... | collective-permute-start | bytes 98312 | tf_op jit(solution)/shard_map/ppermute | solution.py:13
  62.6 29.3 %collective-permute-start.10 = (bf16[16,8,128]{2,1,0:T(8,128)(2,1)S(1)}, bf16[16,8,128]{2,1,0:T(8,128)(2,1)S(1)}, u32[]{:S(2)}, u32[]{:S(2)}) collective-permute-start(bf16[16,8,128]{2,1,0:T(8,128)(2,1)S(1)} %get-tuple-element.44), channel_id=1, source_target_pairs={{15,0},{16,1},{17,2},{18,3},{19,4},{20,5},{21,6},{22,7},{23,8},{24... | collective-permute-start | bytes 98312 | tf_op jit(solution)/shard_map/ppermute | solution.py:13
  64.5 28.7 %collective-permute-start.11 = (bf16[16,8,128]{2,1,0:T(8,128)(2,1)S(1)}, bf16[16,8,128]{2,1,0:T(8,128)(2,1)S(1)}, u32[]{:S(2)}, u32[]{:S(2)}) collective-permute-start(bf16[16,8,128]{2,1,0:T(8,128)(2,1)S(1)} %get-tuple-element.43), channel_id=1, source_target_pairs={{1,0},{2,1},{3,2},{4,3},{5,4},{6,5},{7,6},{8,7},{9,8},{10,9},{11,1... | collective-permute-start | bytes 98312 | tf_op jit(solution)/shard_map/ppermute | solution.py:13
  72.6 20.6 %collective-permute-start.12 = (bf16[16,8,128]{2,1,0:T(8,128)(2,1)S(1)}, bf16[16,8,128]{2,1,0:T(8,128)(2,1)S(1)}, u32[]{:S(2)}, u32[]{:S(2)}) collective-permute-start(bf16[16,8,128]{2,1,0:T(8,128)(2,1)S(1)} %get-tuple-element.42), channel_id=1, source_target_pairs={{0,1},{1,2},{2,3},{3,4},{4,5},{5,6},{6,7},{7,8},{8,9},{9,10},{10,1... | collective-permute-start | bytes 98312 | tf_op jit(solution)/shard_map/ppermute | solution.py:13
  74.5 18.7 %collective-permute-start.13 = (bf16[16,8,128]{2,1,0:T(8,128)(2,1)S(1)}, bf16[16,8,128]{2,1,0:T(8,128)(2,1)S(1)}, u32[]{:S(2)}, u32[]{:S(2)}) collective-permute-start(bf16[16,8,128]{2,1,0:T(8,128)(2,1)S(1)} %get-tuple-element.41), channel_id=1, source_target_pairs={{0,15},{1,16},{2,17},{3,18},{4,19},{5,20},{6,21},{7,22},{8,23},{9,... | collective-permute-start | bytes 98312 | tf_op jit(solution)/shard_map/ppermute | solution.py:13
  84.1 9.2 %collective-permute-start.14 = (bf16[16,8,128]{2,1,0:T(8,128)(2,1)S(1)}, bf16[16,8,128]{2,1,0:T(8,128)(2,1)S(1)}, u32[]{:S(2)}, u32[]{:S(2)}) collective-permute-start(bf16[16,8,128]{2,1,0:T(8,128)(2,1)S(1)} %get-tuple-element.40), channel_id=1, source_target_pairs={{0,16},{1,17},{2,18},{3,19},{4,20},{5,21},{6,22},{7,23},{8,24},{9,... | collective-permute-start | bytes 98312 | tf_op jit(solution)/shard_map/ppermute | solution.py:13
  91.9 2.3 collective-permute-start.15
  97.6 5.9 %copy-start.8 = (f32[64]{0:T(128)S(1)}, f32[64]{0:T(128)}, u32[]{:S(2)}) copy-start(f32[64]{0:T(128)} %copy-done.6) | copy-start | bytes 772
  104.7 0.7 copy-start.3
  108.0 15.7 %collective-permute-start.16 = (bf16[16,8,128]{2,1,0:T(8,128)(2,1)S(1)}, bf16[16,8,128]{2,1,0:T(8,128)(2,1)S(1)}, u32[]{:S(2)}, u32[]{:S(2)}) collective-permute-start(bf16[16,8,128]{2,1,0:T(8,128)(2,1)S(1)} %get-tuple-element.38), channel_id=1, source_target_pairs={{17,0},{18,1},{19,2},{20,3},{21,4},{22,5},{23,6},{24,7},{25,8},{26... | collective-permute-start | bytes 98312 | tf_op jit(solution)/shard_map/ppermute | solution.py:13
  109.8 23.4 %collective-permute-start.17 = (bf16[16,8,128]{2,1,0:T(8,128)(2,1)S(1)}, bf16[16,8,128]{2,1,0:T(8,128)(2,1)S(1)}, u32[]{:S(2)}, u32[]{:S(2)}) collective-permute-start(bf16[16,8,128]{2,1,0:T(8,128)(2,1)S(1)} %get-tuple-element.37), channel_id=1, source_target_pairs={{16,0},{17,1},{18,2},{19,3},{20,4},{21,5},{22,6},{23,7},{24,8},{25... | collective-permute-start | bytes 98312 | tf_op jit(solution)/shard_map/ppermute | solution.py:13
  111.8 29.4 %collective-permute-start.18 = (bf16[16,8,128]{2,1,0:T(8,128)(2,1)S(1)}, bf16[16,8,128]{2,1,0:T(8,128)(2,1)S(1)}, u32[]{:S(2)}, u32[]{:S(2)}) collective-permute-start(bf16[16,8,128]{2,1,0:T(8,128)(2,1)S(1)} %get-tuple-element.36), channel_id=1, source_target_pairs={{15,0},{16,1},{17,2},{18,3},{19,4},{20,5},{21,6},{22,7},{23,8},{24... | collective-permute-start | bytes 98312 | tf_op jit(solution)/shard_map/ppermute | solution.py:13
  113.7 28.8 %collective-permute-start.19 = (bf16[16,8,128]{2,1,0:T(8,128)(2,1)S(1)}, bf16[16,8,128]{2,1,0:T(8,128)(2,1)S(1)}, u32[]{:S(2)}, u32[]{:S(2)}) collective-permute-start(bf16[16,8,128]{2,1,0:T(8,128)(2,1)S(1)} %get-tuple-element.35), channel_id=1, source_target_pairs={{1,0},{2,1},{3,2},{4,3},{5,4},{6,5},{7,6},{8,7},{9,8},{10,9},{11,1... | collective-permute-start | bytes 98312 | tf_op jit(solution)/shard_map/ppermute | solution.py:13
  121.8 20.7 %collective-permute-start.20 = (bf16[16,8,128]{2,1,0:T(8,128)(2,1)S(1)}, bf16[16,8,128]{2,1,0:T(8,128)(2,1)S(1)}, u32[]{:S(2)}, u32[]{:S(2)}) collective-permute-start(bf16[16,8,128]{2,1,0:T(8,128)(2,1)S(1)} %get-tuple-element.34), channel_id=1, source_target_pairs={{0,1},{1,2},{2,3},{3,4},{4,5},{5,6},{6,7},{7,8},{8,9},{9,10},{10,1... | collective-permute-start | bytes 98312 | tf_op jit(solution)/shard_map/ppermute | solution.py:13
  123.7 18.8 %collective-permute-start.21 = (bf16[16,8,128]{2,1,0:T(8,128)(2,1)S(1)}, bf16[16,8,128]{2,1,0:T(8,128)(2,1)S(1)}, u32[]{:S(2)}, u32[]{:S(2)}) collective-permute-start(bf16[16,8,128]{2,1,0:T(8,128)(2,1)S(1)} %get-tuple-element.33), channel_id=1, source_target_pairs={{0,15},{1,16},{2,17},{3,18},{4,19},{5,20},{6,21},{7,22},{8,23},{9,... | collective-permute-start | bytes 98312 | tf_op jit(solution)/shard_map/ppermute | solution.py:13
  133.3 9.3 %collective-permute-start.22 = (bf16[16,8,128]{2,1,0:T(8,128)(2,1)S(1)}, bf16[16,8,128]{2,1,0:T(8,128)(2,1)S(1)}, u32[]{:S(2)}, u32[]{:S(2)}) collective-permute-start(bf16[16,8,128]{2,1,0:T(8,128)(2,1)S(1)} %get-tuple-element.32), channel_id=1, source_target_pairs={{0,16},{1,17},{2,18},{3,19},{4,20},{5,21},{6,22},{7,23},{8,24},{9,... | collective-permute-start | bytes 98312 | tf_op jit(solution)/shard_map/ppermute | solution.py:13
  141.1 2.3 collective-permute-start.23
  146.9 5.9 %copy-start.9 = (f32[64]{0:T(128)S(1)}, f32[64]{0:T(128)}, u32[]{:S(2)}) copy-start(f32[64]{0:T(128)} %copy-done.6) | copy-start | bytes 772
  153.9 0.7 copy-start.4
  157.3 15.7 %collective-permute-start.24 = (bf16[16,8,128]{2,1,0:T(8,128)(2,1)S(1)}, bf16[16,8,128]{2,1,0:T(8,128)(2,1)S(1)}, u32[]{:S(2)}, u32[]{:S(2)}) collective-permute-start(bf16[16,8,128]{2,1,0:T(8,128)(2,1)S(1)} %get-tuple-element.30), channel_id=1, source_target_pairs={{17,0},{18,1},{19,2},{20,3},{21,4},{22,5},{23,6},{24,7},{25,8},{26... | collective-permute-start | bytes 98312 | tf_op jit(solution)/shard_map/ppermute | solution.py:13
  159.1 23.6 %collective-permute-start.25 = (bf16[16,8,128]{2,1,0:T(8,128)(2,1)S(1)}, bf16[16,8,128]{2,1,0:T(8,128)(2,1)S(1)}, u32[]{:S(2)}, u32[]{:S(2)}) collective-permute-start(bf16[16,8,128]{2,1,0:T(8,128)(2,1)S(1)} %get-tuple-element.29), channel_id=1, source_target_pairs={{16,0},{17,1},{18,2},{19,3},{20,4},{21,5},{22,6},{23,7},{24,8},{25... | collective-permute-start | bytes 98312 | tf_op jit(solution)/shard_map/ppermute | solution.py:13
  161.0 29.5 %collective-permute-start.26 = (bf16[16,8,128]{2,1,0:T(8,128)(2,1)S(1)}, bf16[16,8,128]{2,1,0:T(8,128)(2,1)S(1)}, u32[]{:S(2)}, u32[]{:S(2)}) collective-permute-start(bf16[16,8,128]{2,1,0:T(8,128)(2,1)S(1)} %get-tuple-element.28), channel_id=1, source_target_pairs={{15,0},{16,1},{17,2},{18,3},{19,4},{20,5},{21,6},{22,7},{23,8},{24... | collective-permute-start | bytes 98312 | tf_op jit(solution)/shard_map/ppermute | solution.py:13
  162.9 29.1 %collective-permute-start.27 = (bf16[16,8,128]{2,1,0:T(8,128)(2,1)S(1)}, bf16[16,8,128]{2,1,0:T(8,128)(2,1)S(1)}, u32[]{:S(2)}, u32[]{:S(2)}) collective-permute-start(bf16[16,8,128]{2,1,0:T(8,128)(2,1)S(1)} %get-tuple-element.27), channel_id=1, source_target_pairs={{1,0},{2,1},{3,2},{4,3},{5,4},{6,5},{7,6},{8,7},{9,8},{10,9},{11,1... | collective-permute-start | bytes 98312 | tf_op jit(solution)/shard_map/ppermute | solution.py:13
  171.1 21.0 %collective-permute-start.28 = (bf16[16,8,128]{2,1,0:T(8,128)(2,1)S(1)}, bf16[16,8,128]{2,1,0:T(8,128)(2,1)S(1)}, u32[]{:S(2)}, u32[]{:S(2)}) collective-permute-start(bf16[16,8,128]{2,1,0:T(8,128)(2,1)S(1)} %get-tuple-element.26), channel_id=1, source_target_pairs={{0,1},{1,2},{2,3},{3,4},{4,5},{5,6},{6,7},{7,8},{8,9},{9,10},{10,1... | collective-permute-start | bytes 98312 | tf_op jit(solution)/shard_map/ppermute | solution.py:13
  173.0 19.0 %collective-permute-start.29 = (bf16[16,8,128]{2,1,0:T(8,128)(2,1)S(1)}, bf16[16,8,128]{2,1,0:T(8,128)(2,1)S(1)}, u32[]{:S(2)}, u32[]{:S(2)}) collective-permute-start(bf16[16,8,128]{2,1,0:T(8,128)(2,1)S(1)} %get-tuple-element.25), channel_id=1, source_target_pairs={{0,15},{1,16},{2,17},{3,18},{4,19},{5,20},{6,21},{7,22},{8,23},{9,... | collective-permute-start | bytes 98312 | tf_op jit(solution)/shard_map/ppermute | solution.py:13
  182.7 9.5 %collective-permute-start.30 = (bf16[16,8,128]{2,1,0:T(8,128)(2,1)S(1)}, bf16[16,8,128]{2,1,0:T(8,128)(2,1)S(1)}, u32[]{:S(2)}, u32[]{:S(2)}) collective-permute-start(bf16[16,8,128]{2,1,0:T(8,128)(2,1)S(1)} %get-tuple-element.24), channel_id=1, source_target_pairs={{0,16},{1,17},{2,18},{3,19},{4,20},{5,21},{6,22},{7,23},{8,24},{9,... | collective-permute-start | bytes 98312 | tf_op jit(solution)/shard_map/ppermute | solution.py:13
  190.5 2.3 collective-permute-start.31
  196.2 5.9 %copy-start.10 = (f32[64]{0:T(128)S(1)}, f32[64]{0:T(128)}, u32[]{:S(2)}) copy-start(f32[64]{0:T(128)} %copy-done.6) | copy-start | bytes 772
  204.0 95.9 %copy-start.13 = (pred[4,4]{1,0:T(4,128)(4,1)S(1)}, pred[4,4]{1,0:T(4,128)(4,1)}, u32[]{:S(2)}) copy-start(pred[4,4]{1,0:T(4,128)(4,1)} %iota_compare_fusion) | copy-start | bytes 52
  204.0 96.0 %copy-start.12 = (pred[4,4]{1,0:T(4,128)(4,1)S(1)}, pred[4,4]{1,0:T(4,128)(4,1)}, u32[]{:S(2)}) copy-start(pred[4,4]{1,0:T(4,128)(4,1)} %iota_compare_fusion.1) | copy-start | bytes 52
  302.3 5.9 %copy-start.1 = (f32[64,8,128]{2,1,0:T(8,128)S(1)}, f32[64,8,128]{2,1,0:T(8,128)}, u32[]{:S(2)}) copy-start(f32[64,8,128]{2,1,0:T(8,128)} %param.6) | copy-start | bytes 786436
where the time goes:
time: 311 us; the launch traced here: 309 us
  starting transfers between devices  134 us (43%)
  blocking collectives  87.5 us (28%)
  matrix products  38.9 us (13%)
  other arithmetic  22.7 us (7%)
  local copies, waits for them, and re-layouts  20.8 us (7%)
    ppermute x32, starting transfers between devices, passed_along(): return lax.ppermute(block, axis, route)  134 us
    psum x1, blocking collectives, per_device(): gram = lax.psum(local_gram, ('gx', 'gy'))  87.5 us
    dot_general x4, matrix products, per_device(): jnp.einsum('efij,efrj->eri', face_blocks, gathered, preferred_element_typ...  23.5 us
    gather x4, local copies, waits for them, and re-layouts, per_device(): gathered = jnp.where(present[:, :, None, None], lookup[source], zero_half)  10.4 us
  transfers between devices with their start and end apart: 32, of which 4 were waited for; matrix products, arithmetic and copies ran while one was open for 2% of the time, Pallas kernels for 0%

commit v1 on v0

--- a/solution.py
+++ b/solution.py
@@ -83,7 +83,7 @@
         vectors.append((own_part + face_part) * live_mask)
     basis = jnp.stack(vectors)
     local_gram = jnp.einsum("icrn,jcrn->rij", basis, basis, precision=HIGH)
-    gram = lax.psum(local_gram, ("gx", "gy"))
+    gram = jnp.sum(lax.all_gather(local_gram, ("gx", "gy")), axis=0)
     weights = coefficients(gram)
     solution = jnp.einsum("rk,kcrn->crn", weights, basis[:POWERS], precision=HIGH)
     residual = basis[0] - jnp.einsum("rk,kcrn->crn", weights, basis[1:], precision=HIGH)

time: 311 us -> 344 us (1.11); the launches traced: 309 us -> 337 us
  blocking collectives: 87.5 us -> 116 us
    all_gather x0 -> x1, blocking collectives: none -> 116 us  [per_device(): gram = jnp.sum(lax.all_gather(local_gram, ('gx', 'gy')), axis=0)]
    psum x1 -> x0, blocking collectives: 87.5 us -> none  [per_device(): gram = lax.psum(local_gram, ('gx', 'gy'))]
where the time goes in v1:
time: 344 us; the launch traced here: 337 us
  starting transfers between devices  134 us (39%)
  blocking collectives  116 us (34%)
  matrix products  39.3 us (11%)
  other arithmetic  21.6 us (6%)
  local copies, waits for them, and re-layouts  20.8 us (6%)
    ppermute x32, starting transfers between devices, passed_along(): return lax.ppermute(block, axis, route)  134 us
    all_gather x1, blocking collectives, per_device(): gram = jnp.sum(lax.all_gather(local_gram, ('gx', 'gy')), axis=0)  116 us
    dot_general x4, matrix products, per_device(): jnp.einsum('efij,efrj->eri', face_blocks, gathered, preferred_element_typ...  23.5 us
    gather x4, local copies, waits for them, and re-layouts, per_device(): gathered = jnp.where(present[:, :, None, None], lookup[source], zero_half)  10.4 us
  transfers between devices with their start and end apart: 32, of which 4 were waited for; matrix products, arithmetic and copies ran while one was open for 2% of the time, Pallas kernels for 0%

profile of v1, /device:TPU:1, one launch (start us, length us, event | category | flops | bytes accessed | tf_op | source)
XLA Modules:
  0.0 337.2 jit_solution(15114468187207160188)
XLA Ops:
  7.9 5.1 %collective-permute-start.1 = (bf16[16,8,128]{2,1,0:T(8,128)(2,1)}, bf16[16,8,128]{2,1,0:T(8,128)(2,1)}, u32[]{:S(2)}, u32[]{:S(2)}) collective-permute-start(bf16[16,8,128]{2,1,0:T(8,128)(2,1)} %get-tuple-element.53), channel_id=1, source_target_pairs={{16,0},{17,1},{18,2},{19,3},{20,4},{21,5},{22,6},{23,7},{24,8},{25... | collective-permute-start | bytes 98312 | tf_op jit(solution)/shard_map/ppermute | solution.py:13
  13.1 1.9 collective-permute-start.2
  15.0 6.2 %collective-permute-start.3 = (bf16[16,8,128]{2,1,0:T(8,128)(2,1)}, bf16[16,8,128]{2,1,0:T(8,128)(2,1)}, u32[]{:S(2)}, u32[]{:S(2)}) collective-permute-start(bf16[16,8,128]{2,1,0:T(8,128)(2,1)} %get-tuple-element.51), channel_id=1, source_target_pairs={{1,0},{2,1},{3,2},{4,3},{5,4},{6,5},{7,6},{8,7},{9,8},{10,9},{11,1... | collective-permute-start | bytes 98312 | tf_op jit(solution)/shard_map/ppermute | solution.py:13
  21.2 1.9 collective-permute-start.4
  23.2 1.8 constant_dynamic-update-slice_fusion.40
  26.3 8.3 %collective-permute-start.5 = (bf16[16,8,128]{2,1,0:T(8,128)(2,1)}, bf16[16,8,128]{2,1,0:T(8,128)(2,1)S(1)}, u32[]{:S(2)}, u32[]{:S(2)}) collective-permute-start(bf16[16,8,128]{2,1,0:T(8,128)(2,1)} %get-tuple-element.49), channel_id=1, source_target_pairs={{0,15},{1,16},{2,17},{3,18},{4,19},{5,20},{6,21},{7,22},{8,23},{9,... | collective-permute-start | bytes 98312 | tf_op jit(solution)/shard_map/ppermute | solution.py:13
  35.4 6.7 %collective-permute-start.6 = (bf16[16,8,128]{2,1,0:T(8,128)(2,1)}, bf16[16,8,128]{2,1,0:T(8,128)(2,1)S(1)}, u32[]{:S(2)}, u32[]{:S(2)}) collective-permute-start(bf16[16,8,128]{2,1,0:T(8,128)(2,1)} %get-tuple-element.48), channel_id=1, source_target_pairs={{0,16},{1,17},{2,18},{3,19},{4,20},{5,21},{6,22},{7,23},{8,24},{9,... | collective-permute-start | bytes 98312 | tf_op jit(solution)/shard_map/ppermute | solution.py:13
  46.4 2.6 gather_fusion.1
  49.0 5.9 %convolution_bitcast_fusion.3 = f32[64,8,128]{2,1,0:T(8,128)S(1)} fusion(bf16[64,4,128,128]{3,2,1,0:T(8,128)(2,1)} %param.8, bf16[64,4,8,128]{3,2,1,0:T(8,128)(2,1)} %bitcast.296, pred[64,4]{1,0:T(8,128)(4,1)S(1)} %copy.47), kind=kOutput, calls=%fused_computation.21 | convolution fusion | flops 67371008 | bytes 9175296 | tf_op jit(solution)/shard_map/efij,efrj->eri/dot_general | solution.py:80
  56.8 1.4 gather_fusion.2
  59.5 1.3 collective-permute-start.8
  60.8 1.9 collective-permute-start.9
  62.7 1.9 collective-permute-start.10
  64.6 8.1 %collective-permute-start.11 = (bf16[16,8,128]{2,1,0:T(8,128)(2,1)S(1)}, bf16[16,8,128]{2,1,0:T(8,128)(2,1)S(1)}, u32[]{:S(2)}, u32[]{:S(2)}) collective-permute-start(bf16[16,8,128]{2,1,0:T(8,128)(2,1)S(1)} %get-tuple-element.43), channel_id=1, source_target_pairs={{1,0},{2,1},{3,2},{4,3},{5,4},{6,5},{7,6},{8,7},{9,8},{10,9},{11,1... | collective-permute-start | bytes 98312 | tf_op jit(solution)/shard_map/ppermute | solution.py:13
  72.7 1.9 collective-permute-start.12
  74.7 9.5 %collective-permute-start.13 = (bf16[16,8,128]{2,1,0:T(8,128)(2,1)S(1)}, bf16[16,8,128]{2,1,0:T(8,128)(2,1)S(1)}, u32[]{:S(2)}, u32[]{:S(2)}) collective-permute-start(bf16[16,8,128]{2,1,0:T(8,128)(2,1)S(1)} %get-tuple-element.41), channel_id=1, source_target_pairs={{0,15},{1,16},{2,17},{3,18},{4,19},{5,20},{6,21},{7,22},{8,23},{9,... | collective-permute-start | bytes 98312 | tf_op jit(solution)/shard_map/ppermute | solution.py:13
  84.2 7.8 %collective-permute-start.14 = (bf16[16,8,128]{2,1,0:T(8,128)(2,1)S(1)}, bf16[16,8,128]{2,1,0:T(8,128)(2,1)S(1)}, u32[]{:S(2)}, u32[]{:S(2)}) collective-permute-start(bf16[16,8,128]{2,1,0:T(8,128)(2,1)S(1)} %get-tuple-element.40), channel_id=1, source_target_pairs={{0,16},{1,17},{2,18},{3,19},{4,20},{5,21},{6,22},{7,23},{8,24},{9,... | collective-permute-start | bytes 98312 | tf_op jit(solution)/shard_map/ppermute | solution.py:13
  92.0 1.3 collective-permute-start.15
  95.1 2.6 gather_fusion.3
  97.7 5.9 %convolution_bitcast_fusion.2 = f32[64,8,128]{2,1,0:T(8,128)S(1)} fusion(bf16[64,4,128,128]{3,2,1,0:T(8,128)(2,1)} %param.8, bf16[64,4,8,128]{3,2,1,0:T(8,128)(2,1)} %bitcast.297, pred[64,4]{1,0:T(8,128)(4,1)S(1)} %copy.47), kind=kOutput, calls=%fused_computation.18 | convolution fusion | flops 67371008 | bytes 9175296 | tf_op jit(solution)/shard_map/efij,efrj->eri/dot_general | solution.py:80
  105.5 1.4 gather_fusion.4
  108.2 1.3 collective-permute-start.16
  110.0 1.9 collective-permute-start.17
  111.9 1.9 collective-permute-start.18
  113.9 8.1 %collective-permute-start.19 = (bf16[16,8,128]{2,1,0:T(8,128)(2,1)S(1)}, bf16[16,8,128]{2,1,0:T(8,128)(2,1)S(1)}, u32[]{:S(2)}, u32[]{:S(2)}) collective-permute-start(bf16[16,8,128]{2,1,0:T(8,128)(2,1)S(1)} %get-tuple-element.35), channel_id=1, source_target_pairs={{1,0},{2,1},{3,2},{4,3},{5,4},{6,5},{7,6},{8,7},{9,8},{10,9},{11,1... | collective-permute-start | bytes 98312 | tf_op jit(solution)/shard_map/ppermute | solution.py:13
  122.0 1.9 collective-permute-start.20
  123.9 9.5 %collective-permute-start.21 = (bf16[16,8,128]{2,1,0:T(8,128)(2,1)S(1)}, bf16[16,8,128]{2,1,0:T(8,128)(2,1)S(1)}, u32[]{:S(2)}, u32[]{:S(2)}) collective-permute-start(bf16[16,8,128]{2,1,0:T(8,128)(2,1)S(1)} %get-tuple-element.33), channel_id=1, source_target_pairs={{0,15},{1,16},{2,17},{3,18},{4,19},{5,20},{6,21},{7,22},{8,23},{9,... | collective-permute-start | bytes 98312 | tf_op jit(solution)/shard_map/ppermute | solution.py:13
  133.5 7.8 %collective-permute-start.22 = (bf16[16,8,128]{2,1,0:T(8,128)(2,1)S(1)}, bf16[16,8,128]{2,1,0:T(8,128)(2,1)S(1)}, u32[]{:S(2)}, u32[]{:S(2)}) collective-permute-start(bf16[16,8,128]{2,1,0:T(8,128)(2,1)S(1)} %get-tuple-element.32), channel_id=1, source_target_pairs={{0,16},{1,17},{2,18},{3,19},{4,20},{5,21},{6,22},{7,23},{8,24},{9,... | collective-permute-start | bytes 98312 | tf_op jit(solution)/shard_map/ppermute | solution.py:13
  141.3 1.3 collective-permute-start.23
  144.4 2.6 gather_fusion.5
  147.0 5.9 %convolution_bitcast_fusion.1 = f32[64,8,128]{2,1,0:T(8,128)S(1)} fusion(bf16[64,4,128,128]{3,2,1,0:T(8,128)(2,1)} %param.8, bf16[64,4,8,128]{3,2,1,0:T(8,128)(2,1)} %bitcast.298, pred[64,4]{1,0:T(8,128)(4,1)S(1)} %copy.47), kind=kOutput, calls=%fused_computation.15 | convolution fusion | flops 67371008 | bytes 9175296 | tf_op jit(solution)/shard_map/efij,efrj->eri/dot_general | solution.py:80
  154.9 1.4 gather_fusion.6
  157.5 1.3 collective-permute-start.24
  159.3 1.9 collective-permute-start.25
  161.2 1.9 collective-permute-start.26
  163.2 8.2 %collective-permute-start.27 = (bf16[16,8,128]{2,1,0:T(8,128)(2,1)S(1)}, bf16[16,8,128]{2,1,0:T(8,128)(2,1)S(1)}, u32[]{:S(2)}, u32[]{:S(2)}) collective-permute-start(bf16[16,8,128]{2,1,0:T(8,128)(2,1)S(1)} %get-tuple-element.27), channel_id=1, source_target_pairs={{1,0},{2,1},{3,2},{4,3},{5,4},{6,5},{7,6},{8,7},{9,8},{10,9},{11,1... | collective-permute-start | bytes 98312 | tf_op jit(solution)/shard_map/ppermute | solution.py:13
  171.3 1.9 collective-permute-start.28
  173.3 9.6 %collective-permute-start.29 = (bf16[16,8,128]{2,1,0:T(8,128)(2,1)S(1)}, bf16[16,8,128]{2,1,0:T(8,128)(2,1)S(1)}, u32[]{:S(2)}, u32[]{:S(2)}) collective-permute-start(bf16[16,8,128]{2,1,0:T(8,128)(2,1)S(1)} %get-tuple-element.25), channel_id=1, source_target_pairs={{0,15},{1,16},{2,17},{3,18},{4,19},{5,20},{6,21},{7,22},{8,23},{9,... | collective-permute-start | bytes 98312 | tf_op jit(solution)/shard_map/ppermute | solution.py:13
  182.9 7.8 %collective-permute-start.30 = (bf16[16,8,128]{2,1,0:T(8,128)(2,1)S(1)}, bf16[16,8,128]{2,1,0:T(8,128)(2,1)S(1)}, u32[]{:S(2)}, u32[]{:S(2)}) collective-permute-start(bf16[16,8,128]{2,1,0:T(8,128)(2,1)S(1)} %get-tuple-element.24), channel_id=1, source_target_pairs={{0,16},{1,17},{2,18},{3,19},{4,20},{5,21},{6,22},{7,23},{8,24},{9,... | collective-permute-start | bytes 98312 | tf_op jit(solution)/shard_map/ppermute | solution.py:13
  190.7 1.5 collective-permute-start.31
  193.9 2.6 gather_fusion.7
  196.5 5.9 %convolution_bitcast_fusion = f32[64,8,128]{2,1,0:T(8,128)S(1)} fusion(bf16[64,4,128,128]{3,2,1,0:T(8,128)(2,1)} %param.8, bf16[64,4,8,128]{3,2,1,0:T(8,128)(2,1)} %bitcast.295, pred[64,4]{1,0:T(8,128)(4,1)S(1)} %copy.47), kind=kOutput, calls=%fused_computation.11 | convolution fusion | flops 67371008 | bytes 9175296 | tf_op jit(solution)/shard_map/efij,efrj->eri/dot_general | solution.py:80
  202.3 1.9 constant_dynamic-update-slice_fusion.36
  204.2 5.4 %fusion.7 = f32[8,5,5]{2,1,0:T(8,128)S(1)} fusion(f32[5,64,8,128]{3,2,1,0:T(8,128)S(1)} %get-tuple-element.61), kind=kOutput, calls=%fused_computation.24 | convolution fusion | flops 19660800 | bytes 1311520 | tf_op jit(solution)/shard_map/icrn,jcrn->rij/dot_general | solution.py:85
  209.6 116.2 %all-gather = f32[2048,5,5]{2,0,1:T(8,128)S(1)} all-gather(f32[8,5,5]{2,0,1:T(8,128)S(1)} %copy.51), channel_id=2, replica_groups=mesh['gx'=16,'gy'=16] {'gx','gy'}, dimensions={0}, use_global_device_ids=true | all-gather | bytes 205600 | tf_op jit(solution)/shard_map/all_gather | solution.py:86
  326.5 3.0 custom-call.4
  330.5 2.5 fusion.12
  333.8 2.5 fusion.10
  (160 shorter events, 31.9 us)
Async XLA Ops:
  0.6 54.3 %copy-start = (bf16[64,128,128]{2,1,0:T(8,128)(2,1)S(1)}, bf16[64,128,128]{2,1,0:T(8,128)(2,1)}, u32[]{:S(2)}) copy-start(bf16[64,128,128]{2,1,0:T(8,128)(2,1)} %param.7) | copy-start | bytes 6291460
  0.6 24.3 %copy-start.16 = (s32[64,4]{0,1:T(4,128)S(1)}, s32[64,4]{0,1:T(4,128)}, u32[]{:S(2)}) copy-start(s32[64,4]{0,1:T(4,128)} %param.9) | copy-start | bytes 3076
  2.9 22.6 %copy-start.11 = (f32[64]{0:T(128)}, f32[64]{0:T(128)S(1)}, u32[]{:S(2)}) copy-start(f32[64]{0:T(128)S(1)} %compare_convert_fusion) | copy-start | bytes 772
  3.9 17.3 %copy-start.10 = (pred[1,9,16]{2,1,0:T(8,128)(4,1)}, pred[1,9,16]{2,1,0:T(8,128)(4,1)S(1)}, u32[]{:S(2)}) copy-start(pred[1,9,16]{2,1,0:T(8,128)(4,1)S(1)} %copy.91) | copy-start | bytes 436
  6.6 19.7 %collective-permute-start = (bf16[16,8,128]{2,1,0:T(8,128)(2,1)}, bf16[16,8,128]{2,1,0:T(8,128)(2,1)}, u32[]{:S(2)}, u32[]{:S(2)}) collective-permute-start(bf16[16,8,128]{2,1,0:T(8,128)(2,1)} %get-tuple-element.54), channel_id=1, source_target_pairs={{17,0},{18,1},{19,2},{20,3},{21,4},{22,5},{23,6},{24,7},{25,8},{26... | collective-permute-start | bytes 98312 | tf_op jit(solution)/shard_map/ppermute | solution.py:13
  7.9 27.5 %collective-permute-start.1 = (bf16[16,8,128]{2,1,0:T(8,128)(2,1)}, bf16[16,8,128]{2,1,0:T(8,128)(2,1)}, u32[]{:S(2)}, u32[]{:S(2)}) collective-permute-start(bf16[16,8,128]{2,1,0:T(8,128)(2,1)} %get-tuple-element.53), channel_id=1, source_target_pairs={{16,0},{17,1},{18,2},{19,3},{20,4},{21,5},{22,6},{23,7},{24,8},{25... | collective-permute-start | bytes 98312 | tf_op jit(solution)/shard_map/ppermute | solution.py:13
  13.1 29.9 %collective-permute-start.2 = (bf16[16,8,128]{2,1,0:T(8,128)(2,1)}, bf16[16,8,128]{2,1,0:T(8,128)(2,1)}, u32[]{:S(2)}, u32[]{:S(2)}) collective-permute-start(bf16[16,8,128]{2,1,0:T(8,128)(2,1)} %get-tuple-element.52), channel_id=1, source_target_pairs={{15,0},{16,1},{17,2},{18,3},{19,4},{20,5},{21,6},{22,7},{23,8},{24... | collective-permute-start | bytes 98312 | tf_op jit(solution)/shard_map/ppermute | solution.py:13
  15.0 29.3 %collective-permute-start.3 = (bf16[16,8,128]{2,1,0:T(8,128)(2,1)}, bf16[16,8,128]{2,1,0:T(8,128)(2,1)}, u32[]{:S(2)}, u32[]{:S(2)}) collective-permute-start(bf16[16,8,128]{2,1,0:T(8,128)(2,1)} %get-tuple-element.51), channel_id=1, source_target_pairs={{1,0},{2,1},{3,2},{4,3},{5,4},{6,5},{7,6},{8,7},{9,8},{10,9},{11,1... | collective-permute-start | bytes 98312 | tf_op jit(solution)/shard_map/ppermute | solution.py:13
  21.2 23.9 %collective-permute-start.4 = (bf16[16,8,128]{2,1,0:T(8,128)(2,1)}, bf16[16,8,128]{2,1,0:T(8,128)(2,1)}, u32[]{:S(2)}, u32[]{:S(2)}) collective-permute-start(bf16[16,8,128]{2,1,0:T(8,128)(2,1)} %get-tuple-element.50), channel_id=1, source_target_pairs={{0,1},{1,2},{2,3},{3,4},{4,5},{5,6},{6,7},{7,8},{8,9},{9,10},{10,1... | collective-permute-start | bytes 98312 | tf_op jit(solution)/shard_map/ppermute | solution.py:13
  26.3 18.8 %collective-permute-start.5 = (bf16[16,8,128]{2,1,0:T(8,128)(2,1)}, bf16[16,8,128]{2,1,0:T(8,128)(2,1)S(1)}, u32[]{:S(2)}, u32[]{:S(2)}) collective-permute-start(bf16[16,8,128]{2,1,0:T(8,128)(2,1)} %get-tuple-element.49), channel_id=1, source_target_pairs={{0,15},{1,16},{2,17},{3,18},{4,19},{5,20},{6,21},{7,22},{8,23},{9,... | collective-permute-start | bytes 98312 | tf_op jit(solution)/shard_map/ppermute | solution.py:13
  35.4 9.8 %collective-permute-start.6 = (bf16[16,8,128]{2,1,0:T(8,128)(2,1)}, bf16[16,8,128]{2,1,0:T(8,128)(2,1)S(1)}, u32[]{:S(2)}, u32[]{:S(2)}) collective-permute-start(bf16[16,8,128]{2,1,0:T(8,128)(2,1)} %get-tuple-element.48), channel_id=1, source_target_pairs={{0,16},{1,17},{2,18},{3,19},{4,20},{5,21},{6,22},{7,23},{8,24},{9,... | collective-permute-start | bytes 98312 | tf_op jit(solution)/shard_map/ppermute | solution.py:13
  43.0 2.6 collective-permute-start.7
  49.0 5.9 %copy-start.12 = (f32[64]{0:T(128)S(1)}, f32[64]{0:T(128)}, u32[]{:S(2)}) copy-start(f32[64]{0:T(128)} %copy-done.11) | copy-start | bytes 772
  59.5 15.2 %collective-permute-start.8 = (bf16[16,8,128]{2,1,0:T(8,128)(2,1)S(1)}, bf16[16,8,128]{2,1,0:T(8,128)(2,1)S(1)}, u32[]{:S(2)}, u32[]{:S(2)}) collective-permute-start(bf16[16,8,128]{2,1,0:T(8,128)(2,1)S(1)} %get-tuple-element.46), channel_id=1, source_target_pairs={{17,0},{18,1},{19,2},{20,3},{21,4},{22,5},{23,6},{24,7},{25,8},{26... | collective-permute-start | bytes 98312 | tf_op jit(solution)/shard_map/ppermute | solution.py:13
  60.8 23.4 %collective-permute-start.9 = (bf16[16,8,128]{2,1,0:T(8,128)(2,1)S(1)}, bf16[16,8,128]{2,1,0:T(8,128)(2,1)S(1)}, u32[]{:S(2)}, u32[]{:S(2)}) collective-permute-start(bf16[16,8,128]{2,1,0:T(8,128)(2,1)S(1)} %get-tuple-element.45), channel_id=1, source_target_pairs={{16,0},{17,1},{18,2},{19,3},{20,4},{21,5},{22,6},{23,7},{24,8},{25... | collective-permute-start | bytes 98312 | tf_op jit(solution)/shard_map/ppermute | solution.py:13
  62.7 29.3 %collective-permute-start.10 = (bf16[16,8,128]{2,1,0:T(8,128)(2,1)S(1)}, bf16[16,8,128]{2,1,0:T(8,128)(2,1)S(1)}, u32[]{:S(2)}, u32[]{:S(2)}) collective-permute-start(bf16[16,8,128]{2,1,0:T(8,128)(2,1)S(1)} %get-tuple-element.44), channel_id=1, source_target_pairs={{15,0},{16,1},{17,2},{18,3},{19,4},{20,5},{21,6},{22,7},{23,8},{24... | collective-permute-start | bytes 98312 | tf_op jit(solution)/shard_map/ppermute | solution.py:13
  64.6 28.7 %collective-permute-start.11 = (bf16[16,8,128]{2,1,0:T(8,128)(2,1)S(1)}, bf16[16,8,128]{2,1,0:T(8,128)(2,1)S(1)}, u32[]{:S(2)}, u32[]{:S(2)}) collective-permute-start(bf16[16,8,128]{2,1,0:T(8,128)(2,1)S(1)} %get-tuple-element.43), channel_id=1, source_target_pairs={{1,0},{2,1},{3,2},{4,3},{5,4},{6,5},{7,6},{8,7},{9,8},{10,9},{11,1... | collective-permute-start | bytes 98312 | tf_op jit(solution)/shard_map/ppermute | solution.py:13
  72.7 20.6 %collective-permute-start.12 = (bf16[16,8,128]{2,1,0:T(8,128)(2,1)S(1)}, bf16[16,8,128]{2,1,0:T(8,128)(2,1)S(1)}, u32[]{:S(2)}, u32[]{:S(2)}) collective-permute-start(bf16[16,8,128]{2,1,0:T(8,128)(2,1)S(1)} %get-tuple-element.42), channel_id=1, source_target_pairs={{0,1},{1,2},{2,3},{3,4},{4,5},{5,6},{6,7},{7,8},{8,9},{9,10},{10,1... | collective-permute-start | bytes 98312 | tf_op jit(solution)/shard_map/ppermute | solution.py:13
  74.7 18.7 %collective-permute-start.13 = (bf16[16,8,128]{2,1,0:T(8,128)(2,1)S(1)}, bf16[16,8,128]{2,1,0:T(8,128)(2,1)S(1)}, u32[]{:S(2)}, u32[]{:S(2)}) collective-permute-start(bf16[16,8,128]{2,1,0:T(8,128)(2,1)S(1)} %get-tuple-element.41), channel_id=1, source_target_pairs={{0,15},{1,16},{2,17},{3,18},{4,19},{5,20},{6,21},{7,22},{8,23},{9,... | collective-permute-start | bytes 98312 | tf_op jit(solution)/shard_map/ppermute | solution.py:13
  84.2 9.2 %collective-permute-start.14 = (bf16[16,8,128]{2,1,0:T(8,128)(2,1)S(1)}, bf16[16,8,128]{2,1,0:T(8,128)(2,1)S(1)}, u32[]{:S(2)}, u32[]{:S(2)}) collective-permute-start(bf16[16,8,128]{2,1,0:T(8,128)(2,1)S(1)} %get-tuple-element.40), channel_id=1, source_target_pairs={{0,16},{1,17},{2,18},{3,19},{4,20},{5,21},{6,22},{7,23},{8,24},{9,... | collective-permute-start | bytes 98312 | tf_op jit(solution)/shard_map/ppermute | solution.py:13
  92.0 2.3 collective-permute-start.15
  97.7 5.9 %copy-start.13 = (f32[64]{0:T(128)S(1)}, f32[64]{0:T(128)}, u32[]{:S(2)}) copy-start(f32[64]{0:T(128)} %copy-done.11) | copy-start | bytes 772
  108.2 15.7 %collective-permute-start.16 = (bf16[16,8,128]{2,1,0:T(8,128)(2,1)S(1)}, bf16[16,8,128]{2,1,0:T(8,128)(2,1)S(1)}, u32[]{:S(2)}, u32[]{:S(2)}) collective-permute-start(bf16[16,8,128]{2,1,0:T(8,128)(2,1)S(1)} %get-tuple-element.38), channel_id=1, source_target_pairs={{17,0},{18,1},{19,2},{20,3},{21,4},{22,5},{23,6},{24,7},{25,8},{26... | collective-permute-start | bytes 98312 | tf_op jit(solution)/shard_map/ppermute | solution.py:13
  110.0 23.4 %collective-permute-start.17 = (bf16[16,8,128]{2,1,0:T(8,128)(2,1)S(1)}, bf16[16,8,128]{2,1,0:T(8,128)(2,1)S(1)}, u32[]{:S(2)}, u32[]{:S(2)}) collective-permute-start(bf16[16,8,128]{2,1,0:T(8,128)(2,1)S(1)} %get-tuple-element.37), channel_id=1, source_target_pairs={{16,0},{17,1},{18,2},{19,3},{20,4},{21,5},{22,6},{23,7},{24,8},{25... | collective-permute-start | bytes 98312 | tf_op jit(solution)/shard_map/ppermute | solution.py:13
  111.9 29.4 %collective-permute-start.18 = (bf16[16,8,128]{2,1,0:T(8,128)(2,1)S(1)}, bf16[16,8,128]{2,1,0:T(8,128)(2,1)S(1)}, u32[]{:S(2)}, u32[]{:S(2)}) collective-permute-start(bf16[16,8,128]{2,1,0:T(8,128)(2,1)S(1)} %get-tuple-element.36), channel_id=1, source_target_pairs={{15,0},{16,1},{17,2},{18,3},{19,4},{20,5},{21,6},{22,7},{23,8},{24... | collective-permute-start | bytes 98312 | tf_op jit(solution)/shard_map/ppermute | solution.py:13
  113.9 28.8 %collective-permute-start.19 = (bf16[16,8,128]{2,1,0:T(8,128)(2,1)S(1)}, bf16[16,8,128]{2,1,0:T(8,128)(2,1)S(1)}, u32[]{:S(2)}, u32[]{:S(2)}) collective-permute-start(bf16[16,8,128]{2,1,0:T(8,128)(2,1)S(1)} %get-tuple-element.35), channel_id=1, source_target_pairs={{1,0},{2,1},{3,2},{4,3},{5,4},{6,5},{7,6},{8,7},{9,8},{10,9},{11,1... | collective-permute-start | bytes 98312 | tf_op jit(solution)/shard_map/ppermute | solution.py:13
  122.0 20.7 %collective-permute-start.20 = (bf16[16,8,128]{2,1,0:T(8,128)(2,1)S(1)}, bf16[16,8,128]{2,1,0:T(8,128)(2,1)S(1)}, u32[]{:S(2)}, u32[]{:S(2)}) collective-permute-start(bf16[16,8,128]{2,1,0:T(8,128)(2,1)S(1)} %get-tuple-element.34), channel_id=1, source_target_pairs={{0,1},{1,2},{2,3},{3,4},{4,5},{5,6},{6,7},{7,8},{8,9},{9,10},{10,1... | collective-permute-start | bytes 98312 | tf_op jit(solution)/shard_map/ppermute | solution.py:13
  123.9 18.8 %collective-permute-start.21 = (bf16[16,8,128]{2,1,0:T(8,128)(2,1)S(1)}, bf16[16,8,128]{2,1,0:T(8,128)(2,1)S(1)}, u32[]{:S(2)}, u32[]{:S(2)}) collective-permute-start(bf16[16,8,128]{2,1,0:T(8,128)(2,1)S(1)} %get-tuple-element.33), channel_id=1, source_target_pairs={{0,15},{1,16},{2,17},{3,18},{4,19},{5,20},{6,21},{7,22},{8,23},{9,... | collective-permute-start | bytes 98312 | tf_op jit(solution)/shard_map/ppermute | solution.py:13
  133.5 9.3 %collective-permute-start.22 = (bf16[16,8,128]{2,1,0:T(8,128)(2,1)S(1)}, bf16[16,8,128]{2,1,0:T(8,128)(2,1)S(1)}, u32[]{:S(2)}, u32[]{:S(2)}) collective-permute-start(bf16[16,8,128]{2,1,0:T(8,128)(2,1)S(1)} %get-tuple-element.32), channel_id=1, source_target_pairs={{0,16},{1,17},{2,18},{3,19},{4,20},{5,21},{6,22},{7,23},{8,24},{9,... | collective-permute-start | bytes 98312 | tf_op jit(solution)/shard_map/ppermute | solution.py:13
  141.3 2.3 collective-permute-start.23
  147.0 5.9 %copy-start.14 = (f32[64]{0:T(128)S(1)}, f32[64]{0:T(128)}, u32[]{:S(2)}) copy-start(f32[64]{0:T(128)} %copy-done.11) | copy-start | bytes 772
  157.5 15.8 %collective-permute-start.24 = (bf16[16,8,128]{2,1,0:T(8,128)(2,1)S(1)}, bf16[16,8,128]{2,1,0:T(8,128)(2,1)S(1)}, u32[]{:S(2)}, u32[]{:S(2)}) collective-permute-start(bf16[16,8,128]{2,1,0:T(8,128)(2,1)S(1)} %get-tuple-element.30), channel_id=1, source_target_pairs={{17,0},{18,1},{19,2},{20,3},{21,4},{22,5},{23,6},{24,7},{25,8},{26... | collective-permute-start | bytes 98312 | tf_op jit(solution)/shard_map/ppermute | solution.py:13
  159.3 23.6 %collective-permute-start.25 = (bf16[16,8,128]{2,1,0:T(8,128)(2,1)S(1)}, bf16[16,8,128]{2,1,0:T(8,128)(2,1)S(1)}, u32[]{:S(2)}, u32[]{:S(2)}) collective-permute-start(bf16[16,8,128]{2,1,0:T(8,128)(2,1)S(1)} %get-tuple-element.29), channel_id=1, source_target_pairs={{16,0},{17,1},{18,2},{19,3},{20,4},{21,5},{22,6},{23,7},{24,8},{25... | collective-permute-start | bytes 98312 | tf_op jit(solution)/shard_map/ppermute | solution.py:13
  161.2 29.5 %collective-permute-start.26 = (bf16[16,8,128]{2,1,0:T(8,128)(2,1)S(1)}, bf16[16,8,128]{2,1,0:T(8,128)(2,1)S(1)}, u32[]{:S(2)}, u32[]{:S(2)}) collective-permute-start(bf16[16,8,128]{2,1,0:T(8,128)(2,1)S(1)} %get-tuple-element.28), channel_id=1, source_target_pairs={{15,0},{16,1},{17,2},{18,3},{19,4},{20,5},{21,6},{22,7},{23,8},{24... | collective-permute-start | bytes 98312 | tf_op jit(solution)/shard_map/ppermute | solution.py:13
  163.2 29.1 %collective-permute-start.27 = (bf16[16,8,128]{2,1,0:T(8,128)(2,1)S(1)}, bf16[16,8,128]{2,1,0:T(8,128)(2,1)S(1)}, u32[]{:S(2)}, u32[]{:S(2)}) collective-permute-start(bf16[16,8,128]{2,1,0:T(8,128)(2,1)S(1)} %get-tuple-element.27), channel_id=1, source_target_pairs={{1,0},{2,1},{3,2},{4,3},{5,4},{6,5},{7,6},{8,7},{9,8},{10,9},{11,1... | collective-permute-start | bytes 98312 | tf_op jit(solution)/shard_map/ppermute | solution.py:13
  171.3 20.9 %collective-permute-start.28 = (bf16[16,8,128]{2,1,0:T(8,128)(2,1)S(1)}, bf16[16,8,128]{2,1,0:T(8,128)(2,1)S(1)}, u32[]{:S(2)}, u32[]{:S(2)}) collective-permute-start(bf16[16,8,128]{2,1,0:T(8,128)(2,1)S(1)} %get-tuple-element.26), channel_id=1, source_target_pairs={{0,1},{1,2},{2,3},{3,4},{4,5},{5,6},{6,7},{7,8},{8,9},{9,10},{10,1... | collective-permute-start | bytes 98312 | tf_op jit(solution)/shard_map/ppermute | solution.py:13
  173.3 19.0 %collective-permute-start.29 = (bf16[16,8,128]{2,1,0:T(8,128)(2,1)S(1)}, bf16[16,8,128]{2,1,0:T(8,128)(2,1)S(1)}, u32[]{:S(2)}, u32[]{:S(2)}) collective-permute-start(bf16[16,8,128]{2,1,0:T(8,128)(2,1)S(1)} %get-tuple-element.25), channel_id=1, source_target_pairs={{0,15},{1,16},{2,17},{3,18},{4,19},{5,20},{6,21},{7,22},{8,23},{9,... | collective-permute-start | bytes 98312 | tf_op jit(solution)/shard_map/ppermute | solution.py:13
  182.9 9.5 %collective-permute-start.30 = (bf16[16,8,128]{2,1,0:T(8,128)(2,1)S(1)}, bf16[16,8,128]{2,1,0:T(8,128)(2,1)S(1)}, u32[]{:S(2)}, u32[]{:S(2)}) collective-permute-start(bf16[16,8,128]{2,1,0:T(8,128)(2,1)S(1)} %get-tuple-element.24), channel_id=1, source_target_pairs={{0,16},{1,17},{2,18},{3,19},{4,20},{5,21},{6,22},{7,23},{8,24},{9,... | collective-permute-start | bytes 98312 | tf_op jit(solution)/shard_map/ppermute | solution.py:13
  190.7 2.3 collective-permute-start.31
  196.5 5.9 %copy-start.15 = (f32[64]{0:T(128)S(1)}, f32[64]{0:T(128)}, u32[]{:S(2)}) copy-start(f32[64]{0:T(128)} %copy-done.11) | copy-start | bytes 772
  325.9 3.6 %copy-start.18 = (pred[4,4]{1,0:T(4,128)(4,1)S(1)}, pred[4,4]{1,0:T(4,128)(4,1)}, u32[]{:S(2)}) copy-start(pred[4,4]{1,0:T(4,128)(4,1)} %iota_compare_fusion) | copy-start | bytes 52
  325.9 3.8 %copy-start.17 = (pred[4,4]{1,0:T(4,128)(4,1)S(1)}, pred[4,4]{1,0:T(4,128)(4,1)}, u32[]{:S(2)}) copy-start(pred[4,4]{1,0:T(4,128)(4,1)} %iota_compare_fusion.1) | copy-start | bytes 52
  325.9 4.4 %copy-start.3 = (f32[64,8,128]{2,1,0:T(8,128)S(1)}, f32[64,8,128]{2,1,0:T(8,128)}, u32[]{:S(2)}) copy-start(f32[64,8,128]{2,1,0:T(8,128)} %copy-done.2) | copy-start | bytes 786436
  325.9 4.4 %copy-start.5 = (f32[64,8,128]{2,1,0:T(8,128)S(1)}, f32[64,8,128]{2,1,0:T(8,128)}, u32[]{:S(2)}) copy-start(f32[64,8,128]{2,1,0:T(8,128)} %copy-done.4) | copy-start | bytes 786436
  325.9 4.4 %copy-start.7 = (f32[64,8,128]{2,1,0:T(8,128)S(1)}, f32[64,8,128]{2,1,0:T(8,128)}, u32[]{:S(2)}) copy-start(f32[64,8,128]{2,1,0:T(8,128)} %copy-done.6) | copy-start | bytes 786436
  325.9 4.4 %copy-start.8 = (f32[1,64,8,128]{3,2,1,0:T(8,128)S(1)}, f32[1,64,8,128]{3,2,1,0:T(8,128)}, u32[]{:S(2)}) copy-start(f32[1,64,8,128]{3,2,1,0:T(8,128)} %get-tuple-element.62) | copy-start | bytes 786436
  325.9 4.4 %copy-start.9 = (f32[1,64,8,128]{3,2,1,0:T(8,128)S(1)}, f32[1,64,8,128]{3,2,1,0:T(8,128)}, u32[]{:S(2)}) copy-start(f32[1,64,8,128]{3,2,1,0:T(8,128)} %get-tuple-element.20) | copy-start | bytes 786436
  330.4 5.9 %copy-start.1 = (f32[64,8,128]{2,1,0:T(8,128)S(1)}, f32[64,8,128]{2,1,0:T(8,128)}, u32[]{:S(2)}) copy-start(f32[64,8,128]{2,1,0:T(8,128)} %param.6) | copy-start | bytes 786436
  (3 other events, 2.2 us)
